TPU v7x, 128 devices: a whole 4x4x4 slice. The times are simulated.
128 devices in a mesh: song: 2 (over y_lo), seq: 64 (over z, x, y_hi, core).
Axes of the slice: x: 4, y: 4 (y_hi: 2, y_lo: 2; y = y_hi * 2 + y_lo), z: 4, core: 2. Of those that a mesh axis runs over, the one named last changes fastest.
Arguments:
- song_ids: int32 [16384], P(('song', 'seq')), parts along dimension 0, may hold values from 0 to 2047
- table: bfloat16 [2048, 2432], P(None, 'seq'), may hold values from -6 to 6
- position_table: bfloat16 [8192, 2432], P('seq'), may hold values from -4 to 4
- w_qkv: bfloat16 [2, 2432, 1800], replicated, may hold values from -4 to 4
- w_out: bfloat16 [2, 600, 2432], replicated, may hold values from -0.25 to 0.25
Outputs:
- stream_out: bfloat16 [16384, 2432], P(('song', 'seq')), parts along dimension 0
There are 2 independent parts, one for each index of `song`. A program takes and returns all parts, laid end to end along the dimension named above; an argument that names none is the same for every part. Nothing has to cross between parts.
All inputs are finite; a program needn't handle non-finite values.
Results may differ from a plain program's by a relative error of at most 0.0065.
Values may be sent and summed in bfloat16 or wider, within the bound.
No kernel may reach another device: no remote copies, remote signals or barrier semaphores. Data moves between devices by JAX's collectives and lax.ppermute only.
A program may use at most 192 MiB of HBM per device.

v0:
```python
import math
import jax
import jax.numpy as jnp
from jax import lax
from jax.sharding import PartitionSpec as P

HEADS = 4
HEAD = 150
epsilon = 1e-05


def from_behind(value, axis, by):
    length = lax.axis_size(axis)
    pairs = [(i, i + by) for i in range(length) if 0 <= i + by < length]
    return lax.ppermute(value, axis, pairs)


def normalize(residual):
    center_mean = jnp.mean(residual, axis=-1, keepdims=True)
    centered = residual - center_mean
    variance = jnp.mean(centered * centered, axis=-1, keepdims=True)
    return (centered * lax.rsqrt(variance + epsilon)).astype(jnp.bfloat16)


def project(residual, weight):
    joined = jnp.dot(normalize(residual), weight, preferred_element_type=jnp.float32).astype(
        jnp.bfloat16
    )
    return joined.reshape(residual.shape[0], HEADS, 3 * HEAD)


def softmax_rounded(scores):
    top_score = jnp.max(scores, axis=-1, keepdims=True)
    lifted = jnp.exp(scores - top_score)
    return (lifted / jnp.sum(lifted, axis=-1, keepdims=True)).astype(jnp.bfloat16)


def shards(song_ids, table, position_table, w_qkv, w_out):
    inv_root = 1.0 / math.sqrt(HEAD)
    axis_count = lax.axis_size("seq")
    row_index = lax.axis_index("seq")
    all_codes = lax.all_gather(song_ids, "seq", axis=0, tiled=True)
    picked = jnp.take(table, all_codes, axis=0)
    embedded = lax.all_to_all(picked, "seq", split_axis=0, concat_axis=1, tiled=True)
    residual = embedded.astype(jnp.float32) + position_table.astype(jnp.float32)
    local_tokens = residual.shape[0]
    joined = project(residual, w_qkv[0])
    every_row = lax.all_gather(joined[:, :, HEAD:], "seq", axis=0, tiled=True)
    row_grid = every_row.reshape(axis_count, local_tokens, HEADS, 2 * HEAD)
    scores = (
        jnp.einsum(
            "chd,rchd->chr",
            joined[:, :, :HEAD],
            row_grid[..., :HEAD],
            preferred_element_type=jnp.float32,
        )
        * inv_root
    )
    allowed = jnp.arange(axis_count) <= row_index
    probs = softmax_rounded(jnp.where(allowed, scores, -jnp.inf))
    mixed = jnp.einsum(
        "chr,rchd->chd", probs, row_grid[..., HEAD:], preferred_element_type=jnp.float32
    ).astype(jnp.bfloat16)
    residual = residual + jnp.dot(
        mixed.reshape(local_tokens, HEADS * HEAD), w_out[0], preferred_element_type=jnp.float32
    )
    joined = project(residual, w_qkv[1])
    before = from_behind(joined[:, :, HEAD:], "seq", 1)
    query = joined[:, :, :HEAD]
    far_scores = (
        jnp.einsum("chd,khd->hck", query, before[..., :HEAD], preferred_element_type=jnp.float32)
        * inv_root
    )
    far_scores = jnp.where(row_index > 0, far_scores, -jnp.inf)
    own_scores = (
        jnp.einsum(
            "chd,chd->hc", query, joined[:, :, HEAD : 2 * HEAD], preferred_element_type=jnp.float32
        )
        * inv_root
    )
    top_score = jnp.maximum(jnp.max(far_scores, axis=-1), own_scores)
    far_lifted = jnp.exp(far_scores - top_score[..., None])
    own_lifted = jnp.exp(own_scores - top_score)
    total = jnp.sum(far_lifted, axis=-1) + own_lifted
    far_probs = (far_lifted / total[..., None]).astype(jnp.bfloat16)
    own_probs = (own_lifted / total).astype(jnp.bfloat16)
    far_part = jnp.einsum(
        "hck,khd->chd", far_probs, before[..., HEAD:], preferred_element_type=jnp.float32
    )
    own_part = jnp.transpose(own_probs.astype(jnp.float32))[..., None] * joined[
        :, :, 2 * HEAD :
    ].astype(jnp.float32)
    mixed = (far_part + own_part).astype(jnp.bfloat16)
    residual = residual + jnp.dot(
        mixed.reshape(local_tokens, HEADS * HEAD), w_out[1], preferred_element_type=jnp.float32
    )
    return residual.astype(jnp.bfloat16)


def solution(mesh):
    in_specs = (P(("song", "seq")), P(None, "seq"), P("seq", None), P(), P())
    out_specs = P(("song", "seq"), None)
    return jax.shard_map(shards, mesh=mesh, in_specs=in_specs, out_specs=out_specs, check_vma=False)
```

profile of v0, /device:TPU:32, one launch (start us, length us, event | category | flops | bytes accessed | tf_op | source)
XLA Modules:
  0.0 349.5 jit_solution(981527527557596328)
XLA Ops:
  6.5 0.0 all-gather.3.cloned.1.call-start
  6.5 83.1 %all-gather = s32[64,1,128]{2,1,0:T(1,128)S(1)} all-gather(s32[1,1,128]{2,1,0:T(1,128)} %bitcast.80), channel_id=1, replica_groups=mesh['song'=2,'seq'=64] {'seq'}, dimensions={0}, use_global_device_ids=true | all-gather | bytes 33280 | tf_op jit(solution)/shard_map/all_gather | solution.py:42
  89.7 1.2 copy.17
  90.9 24.0 %gather_fusion = bf16[8192,38]{1,0:T(8,128)(2,1)S(1)} fusion(bf16[2048,38]{1,0:T(8,128)(2,1)S(1)} %copy.17, s32[8192]{0:T(1024)S(1)} %fusion.43), kind=kCustom, calls=%fused_computation | custom fusion | bytes 1277952 | tf_op jit(solution)/shard_map/jit(_take)/gather | solution.py:43
  115.0 1.0 copy.18
  116.0 0.1 broadcast_select_fusion
  116.1 31.4 %all_to_all.10 = bf16[64,128,38]{1,2,0:T(8,128)(2,1)S(1)} all-to-all(bf16[64,128,38]{1,2,0:T(8,128)(2,1)S(1)} %broadcast_select_fusion), channel_id=1, replica_groups=mesh['song'=2,'seq'=64] {'seq'}, dimensions={0} | all-to-all | bytes 1245184 | tf_op jit(solution)/shard_map/all_to_all | solution.py:44
  147.5 0.1 convert_bitcast_fusion
  147.6 0.1 reshape.65
  147.7 0.0 copy-start
  147.7 0.4 copy.19
  148.1 0.7 copy-done
  148.7 0.2 fusion.39
  149.0 0.3 multiply_reduce_fusion.3
  149.3 6.2 %fusion.13 = bf16[128,1800]{0,1:T(8,128)(2,1)S(1)} fusion(bf16[2,2432,1800]{1,2,0:T(8,128)(2,1)} %param.8, f32[128]{0:T(128)S(1)} %add_rsqrt_fusion.1, f32[128]{0:T(128)S(1)} %broadcast_multiply_fusion.1, f32[128,2432]{1,0:T(8,128)S(1)} %copy.19, bf16[128,2432]{1,0:T(8,128)(2,1)S(1)} %copy-done), kind=kOutput, calls=%fused_computation.20 | convolution fusion | flops 1122452480 | bytes 11084800 | tf_op jit(solution)/shard_map/dot_general | solution.py:26
  155.5 0.1 reshape.60
  155.6 0.8 slice.59
  156.4 0.0 all-gather.3.cloned.1.call-update
  156.5 117.3 %all-gather.3.cloned.1.call-done = bf16[8192,4,300]{0,2,1:T(8,128)(2,1)} async-done(((bf16[128,4,300]{0,2,1:T(8,128)(2,1)}), bf16[8192,4,300]{0,2,1:T(8,128)(2,1)}) %all-gather.3.cloned.1.call-update) | async-done | bytes 19660816 | tf_op jit(solution)/shard_map/all_gather | solution.py:48
  273.8 27.6 %reshape.61 = bf16[64,128,4,300]{1,0,3,2:T(8,128)(2,1)} reshape(bf16[8192,4,300]{0,2,1:T(8,128)(2,1)} %all-gather.3.cloned.1.call-done) | data formatting | bytes 39321600 | tf_op jit(solution)/shard_map/reshape | solution.py:49
  301.3 6.7 %multiply_reduce_fusion.1 = f32[128,4,64]{0,2,1:T(8,128)S(1)} fusion(bf16[64,128,4,300]{1,0,3,2:T(8,128)(2,1)} %reshape.61, f32[128,4,150]{0,2,1:T(8,128)S(1)} %slice_convert_fusion), kind=kLoop, calls=%fused_computation.4 | loop fusion | flops 14712832 | bytes 10268672 | tf_op jit(solution)/shard_map/chd,rchd->chr/dot_general | solution.py:51
  308.0 0.1 fusion.26
  308.2 8.3 %multiply_reduce_fusion = bf16[128,4,150]{0,2,1:T(8,128)(2,1)S(1)} fusion(bf16[64,128,4,300]{1,0,3,2:T(8,128)(2,1)} %reshape.61, f32[128,4,64]{0,2,1:T(8,128)S(1)} %fusion.26), kind=kLoop, calls=%fused_computation.3 | loop fusion | flops 14668800 | bytes 10115072 | tf_op jit(solution)/shard_map/chr,rchd->chd/dot_general | solution.py:61
  316.6 2.6 fusion.53
  319.2 0.3 multiply_reduce_fusion.2
  319.5 6.2 %fusion.16 = bf16[128,1800]{0,1:T(8,128)(2,1)S(1)} fusion(bf16[2,2432,1800]{1,2,0:T(8,128)(2,1)} %param.8, f32[128,2432]{1,0:T(8,128)S(1)} %get-tuple-element.6, f32[128]{0:T(128)S(1)} %add_rsqrt_fusion, f32[128]{0:T(128)S(1)} %broadcast_multiply_fusion), kind=kOutput, calls=%fused_computation.21 | convolution fusion | flops 1121829888 | bytes 10462208 | tf_op jit(solution)/shard_map/dot_general | solution.py:26
  325.7 0.1 reshape.63
  325.8 0.1 slice.62
  325.9 2.2 collective-permute-start
  328.1 0.1 fusion.31
  328.1 10.5 %collective-permute-done = bf16[128,4,300]{0,2,1:T(8,128)(2,1)S(1)} collective-permute-done((bf16[128,4,300]{0,2,1:T(8,128)(2,1)S(1)}, bf16[128,4,300]{0,2,1:T(8,128)(2,1)S(1)}, u32[]{:S(2)}, u32[]{:S(2)}) %collective-permute-start) | collective-permute-done | bytes 307232 | tf_op jit(solution)/shard_map/ppermute | solution.py:15
  338.6 0.3 fusion.54
  338.9 0.1 fusion.32
  339.0 0.3 fusion.21
  339.3 3.4 fusion.8
  (13 shorter events, 0.2 us)
Async XLA Ops:
  6.5 267.2 %all-gather.3.cloned.1.call-start = ((), (), s32[]{:S(2)}) async-start(), calls=%async_computation.1 | async-start | bytes 20234240 | tf_op jit(solution)/shard_map/all_gather | solution.py:48
  147.7 1.1 copy-start
  325.9 12.7 %collective-permute-start = (bf16[128,4,300]{0,2,1:T(8,128)(2,1)S(1)}, bf16[128,4,300]{0,2,1:T(8,128)(2,1)S(1)}, u32[]{:S(2)}, u32[]{:S(2)}) collective-permute-start(bf16[128,4,300]{0,2,1:T(8,128)(2,1)S(1)} %slice.62), channel_id=1, source_target_pairs={{0,1},{1,2},{2,3},{3,4},{4,5},{5,6},{6,7},{7,8},{8,9},{9,10},{10,1... | collective-permute-start | bytes 921608 | tf_op jit(solution)/shard_map/ppermute | solution.py:15
Sparse Core Ops, SparseCore 0:
  156.5 117.1 all-gather.2
where the time goes:
time: 350 us
  waiting for transfers between devices  128 us (37%)
  blocking collectives  115 us (33%)
  local copies, waits for them, and re-layouts  56.2 us (16%)
  matrix products  18.9 us (5%)
  other arithmetic  16.4 us (5%)
  between operations  13.6 us (4%)
    all_gather x1, waiting for transfers between devices, shards(): every_row = lax.all_gather(joined[:, :, HEAD:], 'seq', axis=0, tiled=True)  117 us
    all_gather x1, blocking collectives, shards(): all_codes = lax.all_gather(song_ids, 'seq', axis=0, tiled=True)  83.1 us
    all_to_all x1, blocking collectives, shards(): lax.all_to_all(picked, 'seq', split_axis=0, concat_axis=1, tiled=True)  31.4 us
    reshape x1, local copies, waits for them, and re-layouts, shards(): row_grid = every_row.reshape(axis_count, local_tokens, HEADS, 2 * HEAD)  27.6 us
    gather x2, local copies, waits for them, and re-layouts, shards(): picked = jnp.take(table, all_codes, axis=0)  25 us
    dot_general x2, matrix products, project(): jnp.dot(normalize(residual), weight, preferred_element_type=jnp.float32)  12.3 us
    ppermute x1, waiting for transfers between devices, from_behind(): return lax.ppermute(value, axis, pairs)  10.5 us
    dot_general x1, other arithmetic, shards(): jnp.einsum('chr,rchd->chd', probs, row_grid[..., HEAD:], preferred_elemen...  8.34 us
  transfers between devices with their start and end apart: 2, of which 2 were waited for; matrix products, arithmetic and copies ran while one was open for 0% of the time, Pallas kernels for 0%

commit v1 on v0

--- a/solution.py
+++ b/solution.py
@@ -41,7 +41,10 @@
     row_index = lax.axis_index("seq")
     all_codes = lax.all_gather(song_ids, "seq", axis=0, tiled=True)
     picked = jnp.take(table, all_codes, axis=0)
-    embedded = lax.all_to_all(picked, "seq", split_axis=0, concat_axis=1, tiled=True)
+    embedded = jnp.concatenate(
+        lax.all_to_all(jnp.stack(jnp.split(picked, lax.axis_size("seq"), axis=0)), "seq", 0, 0),
+        axis=1,
+    )
     residual = embedded.astype(jnp.float32) + position_table.astype(jnp.float32)
     local_tokens = residual.shape[0]
     joined = project(residual, w_qkv[0])

time: 350 us -> 355 us (1.014)
  other arithmetic: 16.4 us -> 20.6 us
    select_n x1, other arithmetic: 0.08 us -> 4.27 us  [shards(): picked = jnp.take(table, all_codes, axis=0)]
    gather x2 -> x1, local copies, waits for them, and re-layouts: 25 us -> 24 us  [shards(): picked = jnp.take(table, all_codes, axis=0)]
where the time goes in v1:
time: 355 us
  waiting for transfers between devices  128 us (36%)
  blocking collectives  115 us (32%)
  local copies, waits for them, and re-layouts  56.8 us (16%)
  other arithmetic  20.6 us (6%)
  matrix products  18.9 us (5%)
  between operations  13.9 us (4%)
    all_gather x1, waiting for transfers between devices, shards(): every_row = lax.all_gather(joined[:, :, HEAD:], 'seq', axis=0, tiled=True)  117 us
    all_gather x1, blocking collectives, shards(): all_codes = lax.all_gather(song_ids, 'seq', axis=0, tiled=True)  83.1 us
    all_to_all x1, blocking collectives, shards(): lax.all_to_all(jnp.stack(jnp.split(picked, lax.axis_size('seq'), axis=0))...  31.4 us
    reshape x1, local copies, waits for them, and re-layouts, shards(): row_grid = every_row.reshape(axis_count, local_tokens, HEADS, 2 * HEAD)  27.6 us
    gather x1, local copies, waits for them, and re-layouts, shards(): picked = jnp.take(table, all_codes, axis=0)  24 us
    dot_general x2, matrix products, project(): jnp.dot(normalize(residual), weight, preferred_element_type=jnp.float32)  12.3 us
    ppermute x1, waiting for transfers between devices, from_behind(): return lax.ppermute(value, axis, pairs)  10.5 us
    dot_general x1, other arithmetic, shards(): jnp.einsum('chr,rchd->chd', probs, row_grid[..., HEAD:], preferred_elemen...  8.34 us
  transfers between devices with their start and end apart: 2, of which 2 were waited for; matrix products, arithmetic and copies ran while one was open for 0% of the time, Pallas kernels for 0%

profile of v1, /device:TPU:32, one launch (start us, length us, event | category | flops | bytes accessed | tf_op | source)
XLA Modules:
  0.0 354.6 jit_solution(16140259333840494726)
XLA Ops:
  6.5 0.0 all-gather.3.cloned.1.call-start
  6.5 83.1 %all-gather = s32[64,1,128]{2,1,0:T(1,128)S(1)} all-gather(s32[1,1,128]{2,1,0:T(1,128)} %bitcast.332), channel_id=1, replica_groups=mesh['song'=2,'seq'=64] {'seq'}, dimensions={0}, use_global_device_ids=true | all-gather | bytes 33280 | tf_op jit(solution)/shard_map/all_gather | solution.py:42
  89.7 1.2 copy.81
  90.9 24.0 %gather_fusion = bf16[8192,38]{1,0:T(8,128)(2,1)S(1)} fusion(bf16[2048,38]{1,0:T(8,128)(2,1)S(1)} %copy.81, s32[8192]{0:T(1024)S(1)} %fusion.43), kind=kCustom, calls=%fused_computation | custom fusion | bytes 1277952 | tf_op jit(solution)/shard_map/jit(_take)/gather | solution.py:43
  115.0 4.3 %broadcast_select_fusion = bf16[8192,38]{1,0:T(8,128)(2,1)S(1)} fusion(bf16[8192,38]{1,0:T(8,128)(2,1)S(1)} %gather_fusion, pred[8192]{0:T(1024)(128)(4,1)S(1)} %compare_and_fusion), kind=kLoop, calls=%fused_computation.22 | loop fusion | flops 311296 | bytes 1253376 | tf_op jit(solution)/shard_map/jit(_take)/select_n | solution.py:43
  120.2 1.0 copy.82
  121.3 31.4 %all_to_all.5 = bf16[64,128,38]{1,2,0:T(8,128)(2,1)S(1)} all-to-all(bf16[64,128,38]{1,2,0:T(8,128)(2,1)S(1)} %copy.82), channel_id=1, replica_groups=mesh['song'=2,'seq'=64] {'seq'}, dimensions={0} | all-to-all | bytes 1245184 | tf_op jit(solution)/shard_map/all_to_all | solution.py:45
  152.6 0.1 convert_bitcast_fusion
  152.7 0.0 copy-start
  152.7 0.1 reshape.58
  152.8 0.4 copy.83
  153.2 0.6 copy-done
  153.8 0.2 fusion.39
  154.0 0.3 multiply_reduce_fusion.3
  154.3 6.2 %fusion.13 = bf16[128,1800]{0,1:T(8,128)(2,1)S(1)} fusion(bf16[2,2432,1800]{1,2,0:T(8,128)(2,1)} %param.8, f32[128]{0:T(128)S(1)} %add_rsqrt_fusion.1, f32[128]{0:T(128)S(1)} %broadcast_multiply_fusion.1, f32[128,2432]{1,0:T(8,128)S(1)} %copy.83, bf16[128,2432]{1,0:T(8,128)(2,1)S(1)} %copy-done), kind=kOutput, calls=%fused_computation.20 | convolution fusion | flops 1122452480 | bytes 11084800 | tf_op jit(solution)/shard_map/dot_general | solution.py:26
  160.5 0.1 reshape.53
  160.7 0.8 slice.59
  161.5 0.0 all-gather.3.cloned.1.call-update
  161.5 117.3 %all-gather.3.cloned.1.call-done = bf16[8192,4,300]{0,2,1:T(8,128)(2,1)} async-done(((bf16[128,4,300]{0,2,1:T(8,128)(2,1)}), bf16[8192,4,300]{0,2,1:T(8,128)(2,1)}) %all-gather.3.cloned.1.call-update) | async-done | bytes 19660816 | tf_op jit(solution)/shard_map/all_gather | solution.py:51
  278.8 27.6 %reshape.54 = bf16[64,128,4,300]{1,0,3,2:T(8,128)(2,1)} reshape(bf16[8192,4,300]{0,2,1:T(8,128)(2,1)} %all-gather.3.cloned.1.call-done) | data formatting | bytes 39321600 | tf_op jit(solution)/shard_map/reshape | solution.py:52
  306.4 6.7 %multiply_reduce_fusion.1 = f32[128,4,64]{0,2,1:T(8,128)S(1)} fusion(bf16[64,128,4,300]{1,0,3,2:T(8,128)(2,1)} %reshape.54, f32[128,4,150]{0,2,1:T(8,128)S(1)} %slice_convert_fusion), kind=kLoop, calls=%fused_computation.4 | loop fusion | flops 14712832 | bytes 10268672 | tf_op jit(solution)/shard_map/chd,rchd->chr/dot_general | solution.py:54
  313.1 0.1 fusion.26
  313.2 8.3 %multiply_reduce_fusion = bf16[128,4,150]{0,2,1:T(8,128)(2,1)S(1)} fusion(bf16[64,128,4,300]{1,0,3,2:T(8,128)(2,1)} %reshape.54, f32[128,4,64]{0,2,1:T(8,128)S(1)} %fusion.26), kind=kLoop, calls=%fused_computation.3 | loop fusion | flops 14668800 | bytes 10115072 | tf_op jit(solution)/shard_map/chr,rchd->chd/dot_general | solution.py:64
  321.6 2.6 fusion.53
  324.3 0.3 multiply_reduce_fusion.2
  324.5 6.2 %fusion.16 = bf16[128,1800]{0,1:T(8,128)(2,1)S(1)} fusion(bf16[2,2432,1800]{1,2,0:T(8,128)(2,1)} %param.8, f32[128,2432]{1,0:T(8,128)S(1)} %get-tuple-element.6, f32[128]{0:T(128)S(1)} %add_rsqrt_fusion, f32[128]{0:T(128)S(1)} %broadcast_multiply_fusion), kind=kOutput, calls=%fused_computation.21 | convolution fusion | flops 1121829888 | bytes 10462208 | tf_op jit(solution)/shard_map/dot_general | solution.py:26
  330.7 0.1 reshape.56
  330.9 0.1 slice.62
  330.9 2.2 collective-permute-start
  333.1 0.1 fusion.31
  333.2 10.5 %collective-permute-done = bf16[128,4,300]{0,2,1:T(8,128)(2,1)S(1)} collective-permute-done((bf16[128,4,300]{0,2,1:T(8,128)(2,1)S(1)}, bf16[128,4,300]{0,2,1:T(8,128)(2,1)S(1)}, u32[]{:S(2)}, u32[]{:S(2)}) %collective-permute-start) | collective-permute-done | bytes 307232 | tf_op jit(solution)/shard_map/ppermute | solution.py:15
  343.7 0.3 fusion.54
  344.0 0.1 fusion.32
  344.1 0.3 fusion.21
  344.4 3.4 fusion.8
  (77 shorter events, 0.9 us)
Async XLA Ops:
  6.5 272.3 %all-gather.3.cloned.1.call-start = ((), (), s32[]{:S(2)}) async-start(), calls=%async_computation.1 | async-start | bytes 20234240 | tf_op jit(solution)/shard_map/all_gather | solution.py:51
  152.7 1.1 copy-start
  330.9 12.7 %collective-permute-start = (bf16[128,4,300]{0,2,1:T(8,128)(2,1)S(1)}, bf16[128,4,300]{0,2,1:T(8,128)(2,1)S(1)}, u32[]{:S(2)}, u32[]{:S(2)}) collective-permute-start(bf16[128,4,300]{0,2,1:T(8,128)(2,1)S(1)} %slice.62), channel_id=1, source_target_pairs={{0,1},{1,2},{2,3},{3,4},{4,5},{5,6},{6,7},{7,8},{8,9},{9,10},{10,1... | collective-permute-start | bytes 921608 | tf_op jit(solution)/shard_map/ppermute | solution.py:15
Sparse Core Ops, SparseCore 0:
  161.6 117.1 all-gather.2
